TPU v7x, 512 devices: a whole 4x8x8 slice. The times are simulated.
512 devices in a mesh: row: 8 (over z), col: 16 (over y, core), vox: 4 (over x).
Axes of the slice: x: 4, y: 8, z: 8, core: 2. Of those that a mesh axis runs over, the one named last changes fastest.
Arguments:
- panel_top: bfloat16 [1024, 1024], P('row', ('col', 'vox')), may hold values from -0.059814453 to 0.059814453
- panel_low: bfloat16 [8192, 1024], P('row', ('col', 'vox')), may hold values from -1.1953125 to 1.1953125
- panel_next: bfloat16 [8192, 1024], P('row', ('col', 'vox')), may hold values from -1.1953125 to 1.1953125
- gram_rest: bfloat16 [8192, 8192], P('row', ('col', 'vox')), may hold values from -18 to 18
- inverses: bfloat16 [2, 1024, 1024], P(None, 'row'), as said below
- right_top: bfloat16 [2, 1024, 8192], P(None, None, ('col', 'vox')), may hold values from -1.796875 to 1.796875
- right_low: bfloat16 [8192, 8192], P('row', ('col', 'vox')), may hold values from -24 to 24
Outputs:
- factor: bfloat16 [2, 8192, 1024], P(None, 'row', ('col', 'vox'))
- solved: bfloat16 [2, 1024, 8192], P(None, None, ('col', 'vox'))
- trailing: float32 [8192, 8192], P('row', ('col', 'vox'))
- residual: float32 [8192, 8192], P('row', ('col', 'vox'))
Inputs may be any that keep to these rules, and one draw needn't show every extreme that they name: Each inverses[k] is lower triangular with diagonal entries from 1 to 2.
All inputs are finite; a program needn't handle non-finite values.
Results may differ from a plain program's by a relative error of at most 0.0057.
Values may be sent and summed in bfloat16 or wider, within the bound.
No kernel may reach another device: no remote copies, remote signals or barrier semaphores. Data moves between devices by JAX's collectives and lax.ppermute only.
A program may use at most 64 MiB of HBM per device.

v0:
```python
import jax
import jax.numpy as jnp
from jax import lax
from jax.sharding import PartitionSpec as P


def spread(block, axis, source):
    block = jnp.where(lax.axis_index(axis) == source, block, jnp.zeros_like(block))
    return lax.psum(block, axis)


def contract(left, right):
    return lax.dot_general(
        left, right, (((1,), (1,)), ((), ())), preferred_element_type=jnp.float32
    )


def per_device(panel_top, panel_low, panel_next, gram_rest, inverses, right_top, right_low):
    col_index = lax.axis_index(("col", "vox"))
    row_index = lax.axis_index("row")
    col_width = panel_low.shape[1]
    top_rows = panel_top.shape[0]
    low_rows = panel_low.shape[0]
    rest_cols = gram_rest.shape[1]
    root_row = col_index * rest_cols // low_rows
    whole_inverses = lax.all_gather(inverses, "row", axis=1, tiled=True)
    own_rows = lax.dynamic_slice_in_dim(whole_inverses, col_index * col_width, col_width, 1)
    rows_used = own_rows[0]
    own_top = contract(lax.all_gather(panel_top, ("col", "vox"), axis=1, tiled=True), rows_used)
    own_low = contract(lax.all_gather(panel_low, ("col", "vox"), axis=1, tiled=True), rows_used)
    first_top, first_low = (
        lax.all_gather(own_top.astype(jnp.bfloat16), ("col", "vox"), axis=1, tiled=True),
        lax.all_gather(own_low.astype(jnp.bfloat16), ("col", "vox"), axis=1, tiled=True),
    )
    outgoing = (
        lax.dynamic_slice_in_dim(
            first_top, col_index * col_width - root_row * top_rows, col_width, 0
        ),
        lax.dynamic_slice_in_dim(
            first_low, col_index * rest_cols - root_row * low_rows, rest_cols, 0
        ),
    )
    owner_top, owner_low = (
        spread(outgoing[0], "row", root_row),
        spread(outgoing[1], "row", root_row),
    )
    updated = (panel_next.astype(jnp.float32) - contract(first_low, owner_top)).astype(jnp.bfloat16)
    rows_used = own_rows[1]
    own_next = contract(lax.all_gather(updated, ("col", "vox"), axis=1, tiled=True), rows_used)
    second_low = lax.all_gather(own_next.astype(jnp.bfloat16), ("col", "vox"), axis=1, tiled=True)
    owner_next = spread(
        lax.dynamic_slice_in_dim(
            second_low, col_index * rest_cols - root_row * low_rows, rest_cols, 0
        ),
        "row",
        root_row,
    )
    trailing = (
        gram_rest.astype(jnp.float32)
        - contract(first_low, owner_low)
        - contract(second_low, owner_next)
    )
    first_solve = jnp.dot(
        whole_inverses[0], right_top[0], preferred_element_type=jnp.float32
    ).astype(jnp.bfloat16)
    top_slice = lax.dynamic_slice_in_dim(right_top[1], row_index * top_rows, top_rows, 0)
    top_part = (
        top_slice.astype(jnp.float32)
        - jnp.dot(first_top, first_solve, preferred_element_type=jnp.float32)
    ).astype(jnp.bfloat16)
    top_new = lax.all_gather(top_part, "row", axis=0, tiled=True)
    second_solve = jnp.dot(whole_inverses[1], top_new, preferred_element_type=jnp.float32).astype(
        jnp.bfloat16
    )
    residual = (
        right_low.astype(jnp.float32)
        - jnp.dot(first_low, first_solve, preferred_element_type=jnp.float32)
        - jnp.dot(second_low, second_solve, preferred_element_type=jnp.float32)
    )
    factor = jnp.stack(
        [
            lax.dynamic_slice_in_dim(first_low, col_index * col_width, col_width, 1),
            lax.dynamic_slice_in_dim(second_low, col_index * col_width, col_width, 1),
        ]
    )
    solved = jnp.stack([first_solve, second_solve])
    return (factor, solved, trailing, residual)


def solution(mesh):
    in_specs = (
        P("row", ("col", "vox")),
        P("row", ("col", "vox")),
        P("row", ("col", "vox")),
        P("row", ("col", "vox")),
        P(None, "row", None),
        P(None, None, ("col", "vox")),
        P("row", ("col", "vox")),
    )
    out_specs = (
        P(None, "row", ("col", "vox")),
        P(None, None, ("col", "vox")),
        P("row", ("col", "vox")),
        P("row", ("col", "vox")),
    )
    return jax.shard_map(
        per_device, mesh=mesh, in_specs=in_specs, out_specs=out_specs, check_vma=False
    )
```

profile of v0, /device:TPU:2, one launch (start us, length us, event | category | flops | bytes accessed | tf_op | source)
XLA Modules:
  0.0 587.9 jit_solution(6978349543570293704)
XLA Ops:
  7.2 0.0 copy-start.7
  7.2 0.0 all-gather.8.cloned.1.call-start
  7.2 0.7 all-gather.8.cloned.1.call-update
  7.9 0.0 all-gather.6.cloned.1.call-start
  8.0 0.7 all-gather.6.cloned.1.call-update
  8.7 0.0 copy-start.6
  8.7 0.0 all-gather.10.cloned.1.call-start
  8.7 88.6 %all-gather.8.cloned.1.call-done = bf16[1024,1024]{0,1:T(8,128)(2,1)} async-done(((bf16[1024,16]{0,1:T(8,128)(2,1)}), bf16[1024,1024]{0,1:T(8,128)(2,1)}) %all-gather.8.cloned.1.call-update) | async-done | bytes 2097168 | tf_op jit(solution)/shard_map/all_gather | solution.py:30
  97.4 59.5 %all-gather.6.cloned.1.call-done = bf16[2,1024,1024]{2,1,0:T(8,128)(2,1)} async-done(((bf16[2,128,1024]{2,1,0:T(8,128)(2,1)}), bf16[2,1024,1024]{2,1,0:T(8,128)(2,1)}) %all-gather.6.cloned.1.call-update) | async-done | bytes 4194320 | tf_op jit(solution)/shard_map/all_gather | solution.py:26
  156.9 2.6 fusion.6
  159.5 0.0 all-gather.10.cloned.1.call-update
  159.5 0.0 all-gather.12.cloned.1.call-start
  159.6 0.0 copy-done.7
  159.6 69.7 %all_gather.27 = bf16[128,1024]{0,1:T(8,128)(2,1)S(1)} all-gather(bf16[128,16]{0,1:T(8,128)(2,1)S(1)} %copy-done.7), channel_id=1, replica_groups=mesh['row'=8,'col'=16,'vox'=4] {'col','vox'}, dimensions={1}, use_global_device_ids=true | all-gather | bytes 266240 | tf_op jit(solution)/shard_map/all_gather | solution.py:29
  229.3 0.9 fusion.7
  230.2 66.4 %all_gather.28 = bf16[128,1024]{0,1:T(8,128)(2,1)S(1)} all-gather(bf16[128,16]{0,1:T(8,128)(2,1)S(1)} %fusion.7), channel_id=1, replica_groups=mesh['row'=8,'col'=16,'vox'=4] {'col','vox'}, dimensions={1}, use_global_device_ids=true | all-gather | bytes 266240 | tf_op jit(solution)/shard_map/all_gather | solution.py:32
  296.6 0.1 dynamic-slice_select_fusion.2
  296.8 31.6 %psum.21 = bf16[16,1024]{0,1:T(8,128)(2,1)S(1)} all-reduce(bf16[16,1024]{0,1:T(8,128)(2,1)S(1)} %dynamic-slice_select_fusion.2), channel_id=1, replica_groups=mesh['row'=8,'col'=16,'vox'=4] {'row'}, use_global_device_ids=true, to_apply=%region_0.1 | all-reduce | flops 16384 | bytes 65536 | tf_op jit(solution)/shard_map/psum | solution.py:9
  328.3 0.0 copy-start.4
  328.4 0.0 all-gather.10.cloned.1.call-done
  328.4 0.0 copy-done.6
  328.4 2.7 fusion.4
  331.1 0.0 all-gather.12.cloned.1.call-update
  331.1 0.0 all-gather.14.cloned.1.call-start
  331.2 80.5 %all-gather.12.cloned.1.call-done = bf16[1024,1024]{0,1:T(8,128)(2,1)} async-done(((bf16[1024,16]{0,1:T(8,128)(2,1)}), bf16[1024,1024]{0,1:T(8,128)(2,1)}) %all-gather.12.cloned.1.call-update) | async-done | bytes 2097168 | tf_op jit(solution)/shard_map/all_gather | solution.py:49
  411.7 2.6 convolution_convert_fusion
  414.3 0.0 all-gather.14.cloned.1.call-update
  414.3 0.0 all-reduce.3.cloned.1.call-start
  414.4 0.0 slice-start
  414.4 0.0 copy-done.4
  414.4 0.0 copy-start.8
  414.4 2.4 fusion.2
  416.9 0.0 slice-done
  416.9 0.3 fusion.5
  417.2 26.8 %all_gather.31 = bf16[1024,128]{1,0:T(8,128)(2,1)S(1)} all-gather(bf16[128,128]{1,0:T(8,128)(2,1)S(1)} %fusion.5), channel_id=1, replica_groups=mesh['row'=8,'col'=16,'vox'=4] {'row'}, dimensions={0}, use_global_device_ids=true | all-gather | bytes 294912 | tf_op jit(solution)/shard_map/all_gather | solution.py:71
  444.0 0.0 copy-done.8
  444.0 0.0 copy-start
  444.0 0.0 copy-start.2
  444.0 0.7 fusion.3
  444.7 0.8 pad_maximum_fusion
  445.5 0.0 copy-done
  445.6 0.8 dynamic-slice_select_fusion.1
  446.3 0.0 copy-done.2
  446.3 0.7 convolution_subtract_fusion.1
  447.1 48.9 %all-gather.14.cloned.1.call-done = bf16[1024,1024]{0,1:T(8,128)(2,1)} async-done(((bf16[1024,16]{0,1:T(8,128)(2,1)}), bf16[1024,1024]{0,1:T(8,128)(2,1)}) %all-gather.14.cloned.1.call-update) | async-done | bytes 2097168 | tf_op jit(solution)/shard_map/all_gather | solution.py:50
  496.0 1.7 dynamic-slice_select_fusion
  497.7 0.0 all-reduce.3.cloned.1.call-update
  497.7 0.8 dynamic-slice_bitcast_fusion.3
  498.4 0.6 pad_maximum_fusion.1
  499.1 0.0 copy-start.3
  499.1 3.2 convolution_subtract_fusion
  502.3 75.4 %all-reduce.3.cloned.1.call-done = (bf16[128,1024]{0,1:T(8,128)(2,1)}, bf16[128,1024]{0,1:T(8,128)(2,1)}) async-done(((bf16[128,1024]{0,1:T(8,128)(2,1)}, bf16[128,1024]{0,1:T(8,128)(2,1)}), (bf16[128,1024]{0,1:T(8,128)(2,1)}, bf16[128,1024]{0,1:T(8,128)(2,1)})) %all-reduce.3.cloned.1.call-update) | async-done | bytes 524304 | tf_op jit(solution)/shard_map/psum | solution.py:9
  577.6 0.0 copy-done.3
  577.6 0.0 copy-start.1
  577.6 0.0 copy-start.5
  577.6 1.8 convolution_subtract_fusion.3
  579.5 0.0 copy-done.1
  579.5 0.0 copy-done.5
  579.5 1.5 convolution_subtract_fusion.2
  (1 shorter events, 0.0 us)
Async XLA Ops:
  7.2 152.4 %copy-start.7 = (bf16[128,16]{0,1:T(8,128)(2,1)S(1)}, bf16[128,16]{0,1:T(8,128)(2,1)}, u32[]{:S(2)}) copy-start(bf16[128,16]{0,1:T(8,128)(2,1)} %param.7) | copy-start | bytes 12292
  7.2 90.2 %all-gather.8.cloned.1.call-start = ((), (), s32[]{:S(2)}) async-start(), calls=%async_computation.1 | async-start | bytes 2129920 | tf_op jit(solution)/shard_map/all_gather | solution.py:30
  7.9 149.0 %all-gather.6.cloned.1.call-start = ((), (), s32[]{:S(2)}) async-start(), calls=%async_computation | async-start | bytes 4718592 | tf_op jit(solution)/shard_map/all_gather | solution.py:26
  8.7 319.7 %copy-start.6 = (bf16[1024,16]{0,1:T(8,128)(2,1)S(1)}, bf16[1024,16]{0,1:T(8,128)(2,1)}, u32[]{:S(2)}) copy-start(bf16[1024,16]{0,1:T(8,128)(2,1)} %param.9) | copy-start | bytes 98308
  8.7 319.7 %all-gather.10.cloned.1.call-start = ((), (), s32[]{:S(2)}) async-start(), calls=%async_computation.2 | async-start | bytes 2129920 | tf_op jit(solution)/shard_map/all_gather | solution.py:33
  159.5 252.2 %all-gather.12.cloned.1.call-start = ((), (), s32[]{:S(2)}) async-start(), calls=%async_computation.3 | async-start | bytes 2129920 | tf_op jit(solution)/shard_map/all_gather | solution.py:49
  328.3 86.1 %copy-start.4 = (bf16[2,1024,128]{2,1,0:T(8,128)(2,1)S(1)}, bf16[2,1024,128]{2,1,0:T(8,128)(2,1)}, u32[]{:S(2)}) copy-start(bf16[2,1024,128]{2,1,0:T(8,128)(2,1)} %param.12) | copy-start | bytes 1572868
  331.1 164.9 %all-gather.14.cloned.1.call-start = ((), (), s32[]{:S(2)}) async-start(), calls=%async_computation.4 | async-start | bytes 2129920 | tf_op jit(solution)/shard_map/all_gather | solution.py:50
  414.3 163.3 %all-reduce.3.cloned.1.call-start = ((), (), s32[]{:S(2)}) async-start(), calls=%async_computation.5 | async-start | bytes 1048576 | tf_op jit(solution)/shard_map/psum | solution.py:9
  414.4 2.5 slice-start
  414.4 29.5 %copy-start.8 = (bf16[2,1024,1024]{2,1,0:T(8,128)(2,1)S(1)}, bf16[2,1024,1024]{2,1,0:T(8,128)(2,1)}, u32[]{:S(2)}) copy-start(bf16[2,1024,1024]{2,1,0:T(8,128)(2,1)} %all-gather.6.cloned.1.call-done) | copy-start | bytes 12582916
  444.0 1.6 copy-start
  444.0 2.4 copy-start.2
  499.1 78.6 %copy-start.3 = (bf16[1024,128]{1,0:T(8,128)(2,1)S(1)}, bf16[1024,128]{1,0:T(8,128)(2,1)}, u32[]{:S(2)}) copy-start(bf16[1024,128]{1,0:T(8,128)(2,1)} %param.10) | copy-start | bytes 786436
  577.6 1.8 copy-start.1
  577.6 1.9 copy-start.5
Sparse Core Ops, SparseCore 0:
  11.4 85.9 all-gather.7
  99.5 57.3 all-gather.5
  160.8 79.4 all-gather.9
  331.2 80.4 all-gather.11
  415.5 80.4 all-gather.13
  498.8 78.8 all-reduce.2
where the time goes:
time: 588 us
  waiting for transfers between devices  354 us (60%)
  blocking collectives  194 us (33%)
  matrix products  19.5 us (3%)
  between operations  14.3 us (2%)
    all_gather x1, waiting for transfers between devices, per_device(): lax.all_gather(panel_low, ('col', 'vox'), axis=1, tiled=True)  88.6 us
    all_gather x1, waiting for transfers between devices, per_device(): lax.all_gather(updated, ('col', 'vox'), axis=1, tiled=True)  80.5 us
    psum x1, waiting for transfers between devices, spread(): return lax.psum(block, axis)  75.4 us
    all_gather x1, blocking collectives, per_device(): lax.all_gather(panel_top, ('col', 'vox'), axis=1, tiled=True)  69.7 us
    all_gather x1, blocking collectives, per_device(): lax.all_gather(own_top.astype(jnp.bfloat16), ('col', 'vox'), axis=1, tile...  66.4 us
    all_gather x1, waiting for transfers between devices, per_device(): whole_inverses = lax.all_gather(inverses, 'row', axis=1, tiled=True)  59.5 us
    all_gather x1, waiting for transfers between devices, per_device(): lax.all_gather(own_next.astype(jnp.bfloat16), ('col', 'vox'), axis=1, til...  48.9 us
    psum x1, blocking collectives, spread(): return lax.psum(block, axis)  31.6 us
  transfers between devices with their start and end apart: 6, of which 5 were waited for; matrix products, arithmetic and copies ran while one was open for 2% of the time, Pallas kernels for 0%

commit v1 on v0

--- a/solution.py
+++ b/solution.py
@@ -6,7 +6,11 @@
 
 def spread(block, axis, source):
     block = jnp.where(lax.axis_index(axis) == source, block, jnp.zeros_like(block))
-    return lax.psum(block, axis)
+
+    def leaf_replace(incoming_x, chip_axis):
+        return jnp.sum(jax.lax.all_gather(incoming_x, axis_name=chip_axis), axis=0)
+
+    return leaf_replace(block, axis)
 
 
 def contract(left, right):

time: 588 us -> 606 us (1.031)
  waiting for transfers between devices: 354 us -> 373 us
    psum x1 -> x0, waiting for transfers between devices: 75.4 us -> none  [spread(): return lax.psum(block, axis)]
    all_gather x0 -> x2, waiting for transfers between devices: none -> 62.8 us  [leaf_replace(): return jnp.sum(jax.lax.all_gather(incoming_x, axis_name=chip_axis), axis=0)]
    all_gather x1, waiting for transfers between devices: 48.9 us -> 80.7 us  [per_device(): lax.all_gather(own_next.astype(jnp.bfloat16), ('col', 'vox'), axis=1, til...]
    psum x1 -> x0, blocking collectives: 31.6 us -> none  [spread(): return lax.psum(block, axis)]
    all_gather x0 -> x1, blocking collectives: none -> 24.9 us  [leaf_replace(): return jnp.sum(jax.lax.all_gather(incoming_x, axis_name=chip_axis), axis=0)]
  transfers between devices with their start and end apart: 6 -> 7, of which waited for: 5 -> 6; matrix products, arithmetic and copies ran while one was open for 2% -> 3% of each run, Pallas kernels for 0% -> 0%
where the time goes in v1:
time: 606 us; the launch traced here: 605 us
  waiting for transfers between devices  373 us (62%)
  blocking collectives  188 us (31%)
  matrix products  16.9 us (3%)
  between operations  14.4 us (2%)
  other arithmetic  7.22 us (1%)
    all_gather x1, waiting for transfers between devices, per_device(): lax.all_gather(panel_low, ('col', 'vox'), axis=1, tiled=True)  88.6 us
    all_gather x1, waiting for transfers between devices, per_device(): lax.all_gather(own_next.astype(jnp.bfloat16), ('col', 'vox'), axis=1, til...  80.7 us
    all_gather x1, waiting for transfers between devices, per_device(): lax.all_gather(updated, ('col', 'vox'), axis=1, tiled=True)  79.7 us
    all_gather x1, blocking collectives, per_device(): lax.all_gather(panel_top, ('col', 'vox'), axis=1, tiled=True)  69.7 us
    all_gather x1, blocking collectives, per_device(): lax.all_gather(own_top.astype(jnp.bfloat16), ('col', 'vox'), axis=1, tile...  66.4 us
    all_gather x2, waiting for transfers between devices, leaf_replace(): return jnp.sum(jax.lax.all_gather(incoming_x, axis_name=chip_axis), axis=0)  62.8 us
    all_gather x1, waiting for transfers between devices, per_device(): whole_inverses = lax.all_gather(inverses, 'row', axis=1, tiled=True)  59.5 us
    all_gather x1, blocking collectives, per_device(): top_new = lax.all_gather(top_part, 'row', axis=0, tiled=True)  27.3 us
  transfers between devices with their start and end apart: 7, of which 6 were waited for; matrix products, arithmetic and copies ran while one was open for 3% of the time, Pallas kernels for 0%

profile of v1, /device:TPU:2, one launch (start us, length us, event | category | flops | bytes accessed | tf_op | source)
XLA Modules:
  0.0 605.3 jit_solution(7562011301278253595)
XLA Ops:
  7.2 0.0 copy-start.7
  7.2 0.0 all-gather.13.cloned.1.call-start
  7.2 0.7 all-gather.13.cloned.1.call-update
  7.9 0.0 all-gather.11.cloned.1.call-start
  8.0 0.7 all-gather.11.cloned.1.call-update
  8.7 0.0 all-gather.15.cloned.1.call-start
  8.7 0.0 copy-start.6
  8.7 88.6 %all-gather.13.cloned.1.call-done = bf16[1024,1024]{0,1:T(8,128)(2,1)} async-done(((bf16[1024,16]{0,1:T(8,128)(2,1)}), bf16[1024,1024]{0,1:T(8,128)(2,1)}) %all-gather.13.cloned.1.call-update) | async-done | bytes 2097168 | tf_op jit(solution)/shard_map/all_gather | solution.py:34
  97.4 59.5 %all-gather.11.cloned.1.call-done = bf16[2,1024,1024]{2,1,0:T(8,128)(2,1)} async-done(((bf16[2,128,1024]{2,1,0:T(8,128)(2,1)}), bf16[2,1024,1024]{2,1,0:T(8,128)(2,1)}) %all-gather.11.cloned.1.call-update) | async-done | bytes 4194320 | tf_op jit(solution)/shard_map/all_gather | solution.py:30
  156.9 2.6 fusion.6
  159.5 0.0 all-gather.15.cloned.1.call-update
  159.5 0.0 all-gather.17.cloned.1.call-start
  159.6 0.0 copy-done.7
  159.6 69.7 %all_gather.45 = bf16[128,1024]{0,1:T(8,128)(2,1)S(1)} all-gather(bf16[128,16]{0,1:T(8,128)(2,1)S(1)} %copy-done.7), channel_id=1, replica_groups=mesh['row'=8,'col'=16,'vox'=4] {'col','vox'}, dimensions={1}, use_global_device_ids=true | all-gather | bytes 266240 | tf_op jit(solution)/shard_map/all_gather | solution.py:33
  229.3 0.9 fusion.7
  230.2 66.4 %all_gather.46 = bf16[128,1024]{0,1:T(8,128)(2,1)S(1)} all-gather(bf16[128,16]{0,1:T(8,128)(2,1)S(1)} %fusion.7), channel_id=1, replica_groups=mesh['row'=8,'col'=16,'vox'=4] {'col','vox'}, dimensions={1}, use_global_device_ids=true | all-gather | bytes 266240 | tf_op jit(solution)/shard_map/all_gather | solution.py:36
  296.6 0.1 dynamic-slice_select_fusion.2
  296.8 0.1 copy.14
  296.9 24.9 %all-gather = bf16[128,1024]{1,0:T(8,128)(2,1)S(1)} all-gather(bf16[16,1024]{1,0:T(8,128)(2,1)S(1)} %copy.14), channel_id=2, replica_groups=mesh['row'=8,'col'=16,'vox'=4] {'row'}, dimensions={0}, use_global_device_ids=true | all-gather | bytes 294912 | tf_op jit(solution)/shard_map/all_gather | solution.py:11
  321.8 0.0 all-gather.15.cloned.1.call-done
  321.9 0.0 copy-done.6
  321.9 0.0 copy-start
  321.9 2.7 fusion.4
  324.6 0.0 all-gather.17.cloned.1.call-update
  324.7 0.0 all-gather.19.cloned.1.call-start
  324.7 0.0 copy-start.5
  324.7 79.7 %all-gather.17.cloned.1.call-done = bf16[1024,1024]{0,1:T(8,128)(2,1)} async-done(((bf16[1024,16]{0,1:T(8,128)(2,1)}), bf16[1024,1024]{0,1:T(8,128)(2,1)}) %all-gather.17.cloned.1.call-update) | async-done | bytes 2097168 | tf_op jit(solution)/shard_map/all_gather | solution.py:53
  404.5 2.6 convolution_convert_fusion
  407.1 0.0 all-gather.19.cloned.1.call-update
  407.1 0.0 all-gather.21.cloned.1.call-start
  407.2 0.0 copy-done
  407.2 0.8 dynamic-slice_select_fusion.1
  407.9 0.0 all-gather.21.cloned.1.call-update
  408.0 0.0 all-gather.23.cloned.1.call-start
  408.0 80.7 %all-gather.19.cloned.1.call-done = bf16[1024,1024]{0,1:T(8,128)(2,1)} async-done(((bf16[1024,16]{0,1:T(8,128)(2,1)}), bf16[1024,1024]{0,1:T(8,128)(2,1)}) %all-gather.19.cloned.1.call-update) | async-done | bytes 2097168 | tf_op jit(solution)/shard_map/all_gather | solution.py:54
  488.7 1.7 dynamic-slice_select_fusion
  490.4 0.0 all-gather.23.cloned.1.call-update
  490.4 0.0 slice-start
  490.5 0.0 copy-done.5
  490.5 0.0 copy-start.8
  490.5 2.4 fusion.2
  492.9 0.0 slice-done
  492.9 0.3 fusion.5
  493.2 27.3 %all_gather.51 = bf16[1024,128]{1,0:T(8,128)(2,1)S(1)} all-gather(bf16[128,128]{1,0:T(8,128)(2,1)S(1)} %fusion.5), channel_id=1, replica_groups=mesh['row'=8,'col'=16,'vox'=4] {'row'}, dimensions={0}, use_global_device_ids=true | all-gather | bytes 294912 | tf_op jit(solution)/shard_map/all_gather | solution.py:75
  520.5 0.7 fusion.3
  521.2 0.8 pad_maximum_fusion
  522.0 0.0 copy-done.3
  522.0 0.7 convolution_subtract_fusion.1
  522.8 20.0 %all-gather.21.cloned.1.call-done = bf16[1024,1024]{0,1:T(8,128)(2,1)} async-done(((bf16[128,1024]{0,1:T(8,128)(2,1)}), bf16[1024,1024]{0,1:T(8,128)(2,1)}) %all-gather.21.cloned.1.call-update) | async-done | bytes 2097168 | tf_op jit(solution)/shard_map/all_gather | solution.py:11
  542.8 2.2 copy.17
  545.0 0.0 copy-start.4
  545.0 1.5 bitcast_reduce_fusion.1
  546.6 0.0 copy-done.4
  546.6 0.0 copy-start.1
  546.6 0.7 convolution_subtract_fusion.3
  547.3 0.8 copy-done.1
  548.2 0.6 pad_maximum_fusion.1
  548.8 1.5 convolution_subtract_fusion
  550.3 42.8 %all-gather.23.cloned.1.call-done = bf16[1024,1024]{0,1:T(8,128)(2,1)} async-done(((bf16[128,1024]{0,1:T(8,128)(2,1)}), bf16[1024,1024]{0,1:T(8,128)(2,1)}) %all-gather.23.cloned.1.call-update) | async-done | bytes 2097168 | tf_op jit(solution)/shard_map/all_gather | solution.py:11
  593.1 2.2 copy.18
  595.3 0.0 copy-start.2
  595.3 1.5 bitcast_reduce_fusion
  596.9 0.0 copy-done.2
  596.9 1.5 convolution_subtract_fusion.2
  (5 shorter events, 0.1 us)
Async XLA Ops:
  7.2 152.4 %copy-start.7 = (bf16[128,16]{0,1:T(8,128)(2,1)S(1)}, bf16[128,16]{0,1:T(8,128)(2,1)}, u32[]{:S(2)}) copy-start(bf16[128,16]{0,1:T(8,128)(2,1)} %param.7) | copy-start | bytes 12292
  7.2 90.2 %all-gather.13.cloned.1.call-start = ((), (), s32[]{:S(2)}) async-start(), calls=%async_computation.1 | async-start | bytes 2129920 | tf_op jit(solution)/shard_map/all_gather | solution.py:34
  7.9 149.0 %all-gather.11.cloned.1.call-start = ((), (), s32[]{:S(2)}) async-start(), calls=%async_computation | async-start | bytes 4718592 | tf_op jit(solution)/shard_map/all_gather | solution.py:30
  8.7 313.2 %all-gather.15.cloned.1.call-start = ((), (), s32[]{:S(2)}) async-start(), calls=%async_computation.2 | async-start | bytes 2129920 | tf_op jit(solution)/shard_map/all_gather | solution.py:37
  8.7 313.2 %copy-start.6 = (bf16[1024,16]{0,1:T(8,128)(2,1)S(1)}, bf16[1024,16]{0,1:T(8,128)(2,1)}, u32[]{:S(2)}) copy-start(bf16[1024,16]{0,1:T(8,128)(2,1)} %param.9) | copy-start | bytes 98308
  159.5 245.0 %all-gather.17.cloned.1.call-start = ((), (), s32[]{:S(2)}) async-start(), calls=%async_computation.3 | async-start | bytes 2129920 | tf_op jit(solution)/shard_map/all_gather | solution.py:53
  321.9 85.3 %copy-start = (bf16[1024,1024]{0,1:T(8,128)(2,1)S(1)}, bf16[1024,1024]{0,1:T(8,128)(2,1)}, u32[]{:S(2)}) copy-start(bf16[1024,1024]{0,1:T(8,128)(2,1)} %all-gather.15.cloned.1.call-done) | copy-start | bytes 6291460
  324.7 164.1 %all-gather.19.cloned.1.call-start = ((), (), s32[]{:S(2)}) async-start(), calls=%async_computation.4 | async-start | bytes 2129920 | tf_op jit(solution)/shard_map/all_gather | solution.py:54
  324.7 165.8 %copy-start.5 = (bf16[2,1024,128]{2,1,0:T(8,128)(2,1)S(1)}, bf16[2,1024,128]{2,1,0:T(8,128)(2,1)}, u32[]{:S(2)}) copy-start(bf16[2,1024,128]{2,1,0:T(8,128)(2,1)} %param.12) | copy-start | bytes 1572868
  407.1 135.7 %all-gather.21.cloned.1.call-start = ((), (), s32[]{:S(2)}) async-start(), calls=%async_computation.5 | async-start | bytes 2359296 | tf_op jit(solution)/shard_map/all_gather | solution.py:11
  408.0 185.1 %all-gather.23.cloned.1.call-start = ((), (), s32[]{:S(2)}) async-start(), calls=%async_computation.6 | async-start | bytes 2359296 | tf_op jit(solution)/shard_map/all_gather | solution.py:11
  490.4 2.5 slice-start
  490.5 30.0 %copy-start.8 = (bf16[2,1024,1024]{2,1,0:T(8,128)(2,1)S(1)}, bf16[2,1024,1024]{2,1,0:T(8,128)(2,1)}, u32[]{:S(2)}) copy-start(bf16[2,1024,1024]{2,1,0:T(8,128)(2,1)} %all-gather.11.cloned.1.call-done) | copy-start | bytes 12582916
  520.5 1.6 copy-start.3
  545.0 1.6 copy-start.4
  546.6 1.6 copy-start.1
  595.3 1.6 copy-start.2
Sparse Core Ops, SparseCore 0:
  11.4 85.9 all-gather.12
  99.5 57.3 all-gather.10
  160.8 79.4 all-gather.14
  324.8 79.6 all-gather.16
  408.2 80.4 all-gather.18
  491.1 51.5 all-gather.20
  545.4 47.6 all-gather.22
